TPU v7x, 128 devices: a whole 4x4x4 slice. The times are simulated.
128 devices in a mesh: grp: 2 (over core), row: 16 (over y, x), col: 4 (over z).
Axes of the slice: x: 4, y: 4, z: 4, core: 2. Of those that a mesh axis runs over, the one named last changes fastest.
Arguments:
- root_inverse: bfloat16 [12288, 12288], P(('grp', 'row'), 'col'), may hold values from -0.0546875 to 0.0546875
- child_inverse: bfloat16 [2, 8192, 8192], P('grp', 'row', 'col'), may hold values from -0.0625 to 0.0625
- coupling: bfloat16 [2, 1536, 8192], P('grp', 'col', 'row'), may hold values from -0.0625 to 0.0625
- child_weights: bfloat16 [2, 8192], P('grp', 'col'), may hold values from 0.5 to 2
- root_weights: bfloat16 [12288], P('col'), may hold values from 0.5 to 2
- parent_blocks: int32 [2, 12], replicated, may hold values from 0 to 95, as said below
Outputs:
- grad_root: bfloat16 [12288, 12288], P(('grp', 'row'), 'col')
- grad_child: bfloat16 [2, 8192, 8192], P('grp', 'row', 'col')
- grad_coupling: bfloat16 [2, 1536, 8192], P('grp', 'col', 'row')
Inputs may be any that keep to these rules, and one draw needn't show every extreme that they name: `parent_blocks`: within one child the 12 blocks are distinct; child 0 always names block 0 and block 12288 // 128 - 1; the two children may share blocks.
All inputs are finite; a program needn't handle non-finite values.
Results may differ from a plain program's by a relative error of at most 0.0059.
Values may be sent and summed in bfloat16 or wider, within the bound.
A program may use at most 128 MiB of HBM per device.

v0:
```python
import jax
import jax.numpy as jnp
from jax import lax
from jax.sharding import PartitionSpec as P

BW = 128


def local(root_inverse, child_inverse, coupling, child_weights, root_weights, parent_blocks):
    col_index = lax.axis_index("col")
    col_count = lax.axis_size("col")
    root_rows, root_cols = root_inverse.shape
    local_blocks = root_cols // BW
    share_cols = coupling.shape[1]
    width = share_cols * col_count
    block_count = width // BW
    highest = lax.Precision.HIGHEST
    offset = parent_blocks - col_index * local_blocks
    block_ids = jnp.arange(local_blocks, dtype=jnp.int32)
    owners = [
        (offset[child][:, None] == block_ids[None, :]).astype(jnp.float32) for child in range(2)
    ]
    root_blocks = root_inverse.astype(jnp.float32).reshape(root_rows, local_blocks, BW)
    picks = []
    for child in range(2):
        taken = jnp.einsum("rkb,jk->rjb", root_blocks, owners[child], precision=highest)
        picks.append(taken.reshape(root_rows, width))
    picked = jnp.stack(picks, axis=1)
    selected = lax.psum(picked.astype(jnp.bfloat16), "col")
    mine = lax.dynamic_slice_in_dim(selected, col_index * share_cols, share_cols, 2)
    margin_part = jnp.concatenate(
        [
            jnp.dot(selected[:, child, :].T, mine[:, child, :], preferred_element_type=jnp.float32)
            for child in range(2)
        ],
        axis=0,
    )
    margin = lax.psum_scatter(margin_part, ("grp", "row"), scatter_dimension=0, tiled=True).astype(
        jnp.bfloat16
    )
    factor = child_inverse[0]
    links = coupling[0]
    weights = child_weights[0].astype(jnp.float32)
    links_all = lax.all_gather(links, "col", axis=0, tiled=True)
    solved = lax.psum_scatter(
        jnp.dot(links_all, factor, preferred_element_type=jnp.float32),
        "row",
        scatter_dimension=0,
        tiled=True,
    ).astype(jnp.bfloat16)
    solved_all = lax.all_gather(solved, "row", axis=0, tiled=True)
    scaled = (solved.astype(jnp.float32) * weights[None, :]).astype(jnp.bfloat16)
    adjoint_t = lax.psum_scatter(
        jnp.dot(solved_all, scaled.T, preferred_element_type=jnp.float32),
        "col",
        scatter_dimension=0,
        tiled=True,
    ).astype(jnp.bfloat16)
    adjoint_cols = lax.all_gather(adjoint_t, ("grp", "row"), axis=1, tiled=True).reshape(
        share_cols, 2, width
    )
    lifted = jnp.stack(
        [
            jnp.dot(
                selected[:, child, :],
                adjoint_cols[:, child, :].T,
                preferred_element_type=jnp.float32,
            )
            for child in range(2)
        ],
        axis=1,
    ).astype(jnp.bfloat16)
    lifted_all = lax.all_gather(lifted, "col", axis=2, tiled=True).reshape(
        root_rows, 2, block_count, BW
    )
    placed = jnp.zeros((root_rows, local_blocks, BW), jnp.float32)
    for child in range(2):
        spread = lifted_all[:, child].astype(jnp.float32)
        placed = placed + jnp.einsum("rjb,jk->rkb", spread, owners[child], precision=highest)
    placed = placed.reshape(root_rows, root_cols)
    root_scale = root_weights.astype(jnp.float32)[None, :]
    grad_root = (2.0 * root_inverse.astype(jnp.float32) * root_scale + 2.0 * placed).astype(
        jnp.bfloat16
    )
    margin_row = lax.all_gather(margin, "col", axis=1, tiled=True)
    pulled = (
        2.0 * jnp.dot(margin_row, solved_all, preferred_element_type=jnp.float32) * weights[None, :]
    ).astype(jnp.bfloat16)
    pulled_all = lax.all_gather(pulled, "row", axis=0, tiled=True)
    grad_links = lax.psum_scatter(
        jnp.dot(pulled_all, factor.T, preferred_element_type=jnp.float32),
        "col",
        scatter_dimension=0,
        tiled=True,
    ).astype(jnp.bfloat16)
    grad_factor = jnp.dot(links_all.T, pulled_all, preferred_element_type=jnp.float32)
    grad_factor = (grad_factor + 2.0 * factor.astype(jnp.float32) * weights[None, :]).astype(
        jnp.bfloat16
    )
    return (grad_root, grad_factor[None], grad_links[None])


def solution(mesh):
    return jax.shard_map(
        local,
        mesh=mesh,
        in_specs=(
            P(("grp", "row"), "col"),
            P("grp", "row", "col"),
            P("grp", "col", "row"),
            P("grp", "col"),
            P("col"),
            P(),
        ),
        out_specs=(P(("grp", "row"), "col"), P("grp", "row", "col"), P("grp", "col", "row")),
        check_vma=False,
    )
```

profile of v0, /device:TPU:0, one launch (start us, length us, event | category | flops | bytes accessed | tf_op | source)
XLA Modules:
  0.0 577.9 jit_solution(17137444513439801942)
XLA Ops:
  7.9 30.9 %all-gather.15.cloned.1.call-done = bf16[1,1536,512]{2,1,0:T(8,128)(2,1)} async-done(((bf16[1,384,512]{2,1,0:T(8,128)(2,1)}), bf16[1,1536,512]{2,1,0:T(8,128)(2,1)}) %all-gather.15.cloned.1.call-update) | async-done | bytes 1572880 | tf_op jit(solution)/shard_map/all_gather | solution.py:44
  38.8 10.0 %fusion.6 = f32[1536,2048]{1,0:T(8,128)} fusion(bf16[1,512,2048]{2,1,0:T(8,128)(2,1)} %param.7, bf16[1,1536,512]{2,1,0:T(8,128)(2,1)} %all-gather.15.cloned.1.call-done), kind=kOutput, calls=%fused_computation.12 | convolution fusion | flops 3221225472 | bytes 16252928 | tf_op jit(solution)/shard_map/dot_general | solution.py:46
  48.9 94.8 %reduce-scatter.5.cloned.1.call-done = f32[96,2048]{1,0:T(8,128)} async-done(((f32[1536,2048]{1,0:T(8,128)}), f32[96,2048]{1,0:T(8,128)}) %reduce-scatter.5.cloned.1.call-update) | async-done | bytes 786448 | tf_op jit(solution)/shard_map/reduce_scatter | solution.py:45
  143.8 1.9 convert_element_type.47
  145.8 2.2 copy.20
  148.6 1.8 fusion.13
  150.4 2.1 copy.11
  152.6 1.8 fusion.14
  154.4 2.2 copy.12
  156.5 1.7 pad_maximum_fusion.1
  158.9 47.8 %all-gather.7.cloned.1.call-done = bf16[1536,2048]{1,0:T(8,128)(2,1)} async-done(((bf16[96,2048]{1,0:T(8,128)(2,1)}), bf16[1536,2048]{1,0:T(8,128)(2,1)}) %all-gather.7.cloned.1.call-update) | async-done | bytes 6291472 | tf_op jit(solution)/shard_map/all_gather | solution.py:51
  206.7 5.7 fusion.19
  212.4 60.0 %all-reduce.2.cloned.1.call-done = bf16[384,2,1536]{0,2,1:T(8,128)(2,1)} async-done(((bf16[384,2,1536]{0,2,1:T(8,128)(2,1)}), bf16[384,2,1536]{0,2,1:T(8,128)(2,1)}) %all-reduce.2.cloned.1.call-update) | async-done | bytes 2359312 | tf_op jit(solution)/shard_map/psum | solution.py:29
  272.4 2.4 fusion.17
  275.7 2.5 pad_maximum_fusion
  278.3 18.6 %reduce-scatter.7.cloned.1.call-done = f32[384,96]{0,1:T(8,128)} async-done(((f32[1536,96]{0,1:T(8,128)}), f32[384,96]{0,1:T(8,128)}) %reduce-scatter.7.cloned.1.call-update) | async-done | bytes 147472 | tf_op jit(solution)/shard_map/reduce_scatter | solution.py:53
  298.6 85.4 %reduce-scatter.9.cloned.1.call-done = f32[96,384]{1,0:T(8,128)} async-done(((f32[3072,384]{1,0:T(8,128)}), f32[96,384]{1,0:T(8,128)}) %reduce-scatter.9.cloned.1.call-update) | async-done | bytes 147472 | tf_op jit(solution)/shard_map/reduce_scatter | solution.py:38
  384.9 13.0 %all_gather.22 = bf16[96,1536]{1,0:T(8,128)(2,1)S(1)} all-gather(bf16[96,384]{1,0:T(8,128)(2,1)S(1)} %convert_element_type.52), channel_id=1, replica_groups=mesh['grp'=2,'row'=16,'col'=4] {'col'}, dimensions={1}, use_global_device_ids=true | all-gather | bytes 368640 | tf_op jit(solution)/shard_map/all_gather | solution.py:85
  397.9 4.7 fusion.3
  402.9 27.0 %all-gather.9.cloned.1.call-done = bf16[384,3072]{0,1:T(8,128)(2,1)} async-done(((bf16[384,96]{0,1:T(8,128)(2,1)}), bf16[384,3072]{0,1:T(8,128)(2,1)}) %all-gather.9.cloned.1.call-update) | async-done | bytes 2359312 | tf_op jit(solution)/shard_map/all_gather | solution.py:59
  429.9 2.2 fusion.15
  433.9 59.3 %all-gather.13.cloned.1.call-done = bf16[1536,2048]{1,0:T(8,128)(2,1)} async-done(((bf16[96,2048]{1,0:T(8,128)(2,1)}), bf16[1536,2048]{1,0:T(8,128)(2,1)}) %all-gather.13.cloned.1.call-update) | async-done | bytes 6291472 | tf_op jit(solution)/shard_map/all_gather | solution.py:89
  493.2 8.6 %fusion.4 = f32[1536,512]{1,0:T(8,128)} fusion(bf16[1536,2048]{1,0:T(8,128)(2,1)} %all-gather.13.cloned.1.call-done, bf16[1,512,2048]{2,1,0:T(8,128)(2,1)} %param.7), kind=kOutput, calls=%fused_computation.10 | convolution fusion | flops 3221225472 | bytes 11534336 | tf_op jit(solution)/shard_map/dot_general | solution.py:91
  503.4 2.5 copy.13
  505.9 22.5 %all-gather.11.cloned.1.call-done = bf16[384,2,1536]{2,0,1:T(8,128)(2,1)} async-done(((bf16[384,2,384]{2,0,1:T(8,128)(2,1)}), bf16[384,2,1536]{2,0,1:T(8,128)(2,1)}) %all-gather.11.cloned.1.call-update) | async-done | bytes 2359312 | tf_op jit(solution)/shard_map/all_gather | solution.py:73
  528.4 3.0 copy.14
  534.1 2.3 copy.19
  539.5 2.9 fusion
  542.4 3.7 fusion.2
  546.1 2.4 copy.17
  548.5 20.6 %reduce-scatter.11.cloned.1.call-done = f32[384,512]{1,0:T(8,128)} async-done(((f32[1536,512]{1,0:T(8,128)}), f32[384,512]{1,0:T(8,128)}) %reduce-scatter.11.cloned.1.call-update) | async-done | bytes 786448 | tf_op jit(solution)/shard_map/reduce_scatter | solution.py:90
  569.1 1.9 convert_bitcast_fusion
  (67 shorter events, 14.9 us)
Async XLA Ops:
  7.2 31.7 %all-gather.15.cloned.1.call-start = ((), (), s32[]{:S(2)}) async-start(), calls=%async_computation.13 | async-start | bytes 1966080 | tf_op jit(solution)/shard_map/all_gather | solution.py:44
  7.9 135.9 %reduce-scatter.5.cloned.1.call-start = ((), (), s32[]{:S(2)}) async-start(), calls=%async_computation.5 | async-start | bytes 13369344 | tf_op jit(solution)/shard_map/reduce_scatter | solution.py:45
  48.9 157.8 %all-gather.7.cloned.1.call-start = ((), (), s32[]{:S(2)}) async-start(), calls=%async_computation.6 | async-start | bytes 6684672 | tf_op jit(solution)/shard_map/all_gather | solution.py:51
  145.7 126.7 %all-reduce.2.cloned.1.call-start = ((), (), s32[]{:S(2)}) async-start(), calls=%async_computation.4 | async-start | bytes 4718592 | tf_op jit(solution)/shard_map/psum | solution.py:29
  145.8 2.3 copy-start.11
  148.1 0.6 copy-start.9
  158.2 0.7 copy-start.7
  158.2 48.5 %copy-start.1 = (bf16[96,2048]{1,0:T(8,128)(2,1)S(1)}, bf16[96,2048]{1,0:T(8,128)(2,1)}, u32[]{:S(2)}) copy-start(bf16[96,2048]{1,0:T(8,128)(2,1)} %convert_element_type.47) | copy-start | bytes 1179652
  158.2 138.7 %reduce-scatter.7.cloned.1.call-start = ((), (), s32[]{:S(2)}) async-start(), calls=%async_computation.7 | async-start | bytes 737280 | tf_op jit(solution)/shard_map/reduce_scatter | solution.py:53
  212.4 171.6 %reduce-scatter.9.cloned.1.call-start = ((), (), s32[]{:S(2)}) async-start(), calls=%async_computation.10 | async-start | bytes 4866048 | tf_op jit(solution)/shard_map/reduce_scatter | solution.py:38
  272.4 2.4 copy-start.2
  278.3 151.6 %all-gather.9.cloned.1.call-start = ((), (), s32[]{:S(2)}) async-start(), calls=%async_computation.8 | async-start | bytes 2433024 | tf_op jit(solution)/shard_map/all_gather | solution.py:59
  298.5 194.7 %all-gather.13.cloned.1.call-start = ((), (), s32[]{:S(2)}) async-start(), calls=%async_computation.11 | async-start | bytes 6684672 | tf_op jit(solution)/shard_map/all_gather | solution.py:89
  298.6 104.1 %copy-start.5 = (f32[2048]{0:T(1024)}, f32[2048]{0:T(1024)S(1)}, u32[]{:S(2)}) copy-start(f32[2048]{0:T(1024)S(1)} %broadcast_multiply_fusion) | copy-start | bytes 24580
  402.7 125.7 %all-gather.11.cloned.1.call-start = ((), (), s32[]{:S(2)}) async-start(), calls=%async_computation.9 | async-start | bytes 2949120 | tf_op jit(solution)/shard_map/all_gather | solution.py:73
  429.9 2.2 copy-start.12
  433.9 135.2 %reduce-scatter.11.cloned.1.call-start = ((), (), s32[]{:S(2)}) async-start(), calls=%async_computation.12 | async-start | bytes 3932160 | tf_op jit(solution)/shard_map/reduce_scatter | solution.py:90
  501.8 1.6 copy-start.3
  503.4 2.5 copy-start.8
  534.1 2.3 copy-start.10
  536.5 5.9 %slice-start = ((s8[6291456]{0:T(1024)(128)(4,1)}), s8[4194304]{0:T(1024)(128)(4,1)S(1)}, s32[]{:S(2)}) async-start(s8[6291456]{0:T(1024)(128)(4,1)} %bitcast.102), calls=%async_computation.14 | async-start | bytes 8388608
  537.4 2.1 copy-start
  537.4 5.0 slice-start.1
  539.5 2.9 copy-start.4
  539.5 2.9 copy-start.6
  539.5 2.9 copy-start.13
Sparse Core Ops, SparseCore 0:
  9.6 29.1 all-gather.14
  49.0 94.7 reduce-scatter.4
  146.5 60.1 all-gather.6
  209.5 62.8 all-reduce.1
  275.3 21.6 reduce-scatter.6
  300.5 83.3 reduce-scatter.8
  386.8 43.0 all-gather.8
  432.6 60.5 all-gather.12
  495.5 32.8 all-gather.10
  530.7 38.4 reduce-scatter.10
where the time goes:
time: 579 us; the launch traced here: 578 us
  waiting for transfers between devices  468 us (81%)
  matrix products  44.4 us (8%)
  local copies, waits for them, and re-layouts  23.4 us (4%)
  between operations  14.4 us (2%)
  other arithmetic  14.3 us (2%)
  blocking collectives  13 us (2%)
    reduce_scatter x1, waiting for transfers between devices, local(): lax.psum_scatter(jnp.dot(links_all, factor, preferred_element_type=jnp.fl...  94.8 us
    reduce_scatter x1, waiting for transfers between devices, local(): lax.psum_scatter(margin_part, ('grp', 'row'), scatter_dimension=0, tiled=...  85.4 us
    psum x1, waiting for transfers between devices, local(): selected = lax.psum(picked.astype(jnp.bfloat16), 'col')  60 us
    all_gather x1, waiting for transfers between devices, local(): pulled_all = lax.all_gather(pulled, 'row', axis=0, tiled=True)  59.3 us
    all_gather x1, waiting for transfers between devices, local(): solved_all = lax.all_gather(solved, 'row', axis=0, tiled=True)  47.8 us
    all_gather x1, waiting for transfers between devices, local(): links_all = lax.all_gather(links, 'col', axis=0, tiled=True)  30.9 us
    all_gather x1, waiting for transfers between devices, local(): lax.all_gather(adjoint_t, ('grp', 'row'), axis=1, tiled=True)  27 us
    all_gather x1, waiting for transfers between devices, local(): lax.all_gather(lifted, 'col', axis=2, tiled=True)  22.5 us
  transfers between devices with their start and end apart: 10, of which 10 were waited for; matrix products, arithmetic and copies ran while one was open for 11% of the time, Pallas kernels for 0%

commit v1 on v0

v1 whole, which is shorter than its diff:
```python
import functools

import jax
import jax.numpy as jnp
from jax import lax
from jax.experimental import pallas as pl
from jax.experimental.pallas import tpu as pltpu
from jax.sharding import PartitionSpec as P

BW = 128
MESH = pl.DeviceIdType.MESH
VMEM = pl.BlockSpec(memory_space=pltpu.VMEM)
SMEM = pl.BlockSpec(memory_space=pltpu.SMEM)
F32 = jnp.float32
BF16 = jnp.bfloat16


def ring(i, step):
    return lax.rem(i + step, 4)


class Place:
    def __init__(self):
        row = lax.axis_index("row")
        self.x = lax.rem(row, 4)
        self.y = row // 4
        self.z = lax.axis_index("col")
        self.core = lax.axis_index("grp")
        self.sibling = {"grp": 1 - self.core}
        self.axes = {
            "x": (self.x, [{"row": self.y * 4 + ring(self.x, s)} for s in (1, 3)]),
            "y": (self.y, [{"row": ring(self.y, s) * 4 + self.x} for s in (1, 3)]),
            "z": (self.z, [{"col": ring(self.z, s)} for s in (1, 3)]),
        }

    def meet(self, with_sibling):
        barrier = pltpu.get_barrier_semaphore()
        others = [dev for _, devs in self.axes.values() for dev in devs]
        if with_sibling:
            others.append(self.sibling)
        for dev in others:
            pl.semaphore_signal(barrier, inc=1, device_id=dev, device_id_type=MESH)
        pl.semaphore_wait(barrier, len(others))


class Net:
    def __init__(self, send, recv):
        self.send, self.recv, self.made = send, recv, []

    def copy(self, src, dst, dev):
        at = len(self.made)
        made = pltpu.make_async_remote_copy(
            src_ref=src,
            dst_ref=dst,
            send_sem=self.send.at[at],
            recv_sem=self.recv.at[at],
            device_id=dev,
            device_id_type=MESH,
        )
        self.made.append(made)
        return made

    def drain(self):
        for made in self.made:
            made.wait_send()


class Gather:
    def __init__(self, net, axis, view, own=None):
        me, (right, left) = axis
        lo, hi = ring(me, 3), ring(me, 1)
        own = view(me, None) if own is None else own
        self.first = [net.copy(own, view(me, None), right), net.copy(own, view(me, None), left)]
        self.second = [
            net.copy(view(lo, 0), view(lo, 0), right),
            net.copy(view(hi, 1), view(hi, 1), left),
        ]

    def start(self):
        for copy in self.first:
            copy.start()

    def relay(self):
        for came, goes in zip(self.first, self.second):
            came.wait_recv()
            goes.start()

    def finish(self):
        for copy in self.second:
            copy.wait_recv()


def add_to(ref, other):
    if len(ref.shape) == 2:
        ref[...] = (ref[...].astype(F32) + other[...].astype(F32)).astype(BF16)
        return

    def body(i, _):
        ref[i] = (ref[i].astype(F32) + other[i].astype(F32)).astype(BF16)
        return 0

    lax.fori_loop(0, ref.shape[0], body, 0)


class Scatter:
    def __init__(self, net, axis, view, relay, fin):
        me, (right, left) = axis
        up, down, far = ring(me, 1), ring(me, 3), ring(me, 2)
        self.far = [net.copy(view(far, 0), relay(0), right), net.copy(view(far, 1), relay(1), left)]
        self.near = [
            net.copy(view(up, 1), fin(0, 1), right),
            net.copy(view(down, 0), fin(1, 0), left),
        ]
        self.last = [
            net.copy(relay(0), fin(0, 0), right),
            net.copy(relay(1), fin(1, 1), left),
        ]
        self.adds = [(relay(0), view(up, 0)), (relay(1), view(down, 1))]

    def start(self):
        for copy in self.far + self.near:
            copy.start()

    def relay(self):
        for came, goes, add in zip(self.far, self.last, self.adds):
            came.wait_recv()
            add_to(*add)
            goes.start()

    def finish(self):
        for copy in self.near + self.last:
            copy.wait_recv()


def total(*terms):
    out = terms[0].astype(F32)
    for term in terms[1:]:
        out = out + term.astype(F32)
    return out.astype(BF16)


class GridGather:
    def __init__(self, net, place, buf):
        rows, cols = buf.shape[2:]
        cut = (cols // BW + 1) // 2 * BW
        wide = [pl.ds(0, cut), pl.ds(cut, cols - cut)]
        pair = [pl.ds(0, 2), pl.ds(2, 2)]
        top, low = pl.ds(0, rows // 2), pl.ds(rows // 2, rows // 2)
        x, y = place.x, place.y

        def x_first(i, part):
            return buf.at[y, i, top, :] if part is None else buf.at[y, i, top, wide[part]]

        def y_second(i, part):
            return buf.at[i, :, top, :] if part is None else buf.at[i, pair[part], top, :]

        def y_first(i, part):
            return buf.at[i, x, low, :] if part is None else buf.at[i, x, low, wide[part]]

        def x_second(i, part):
            return buf.at[:, i, low, :] if part is None else buf.at[pair[part], i, low, :]

        self.one = [
            Gather(net, place.axes["x"], x_first),
            Gather(net, place.axes["y"], y_first),
        ]
        self.two = [
            Gather(net, place.axes["y"], y_second),
            Gather(net, place.axes["x"], x_second),
        ]

    def start(self):
        for ring_ in self.one:
            ring_.start()

    def relay(self):
        for ring_ in self.one:
            ring_.relay()

    def turn(self):
        for before, after in zip(self.one, self.two):
            before.finish()
            after.start()

    def relay_two(self):
        for ring_ in self.two:
            ring_.relay()

    def finish(self):
        for ring_ in self.two:
            ring_.finish()


def grid_scatter_scratch(rows, cols):
    half = rows // 2
    cut = (cols // BW + 1) // 2 * BW
    return [
        pltpu.VMEM((2, 2, 2, half, cols), BF16),
        pltpu.VMEM((2, 2, 4, half, cols), BF16),
        pltpu.VMEM((2, 4, half, cols), BF16),
        pltpu.VMEM((2, half, cut), BF16),
        pltpu.VMEM((2, half, cols - cut), BF16),
        pltpu.VMEM((2, 2, half, cols), BF16),
    ]


class GridScatter:
    def __init__(self, net, place, buf, scratch):
        far, fin, mid, far_a, far_b, fin_two = scratch
        rows, cols = buf.shape[2:]
        self.half = half = rows // 2
        cut = (cols // BW + 1) // 2 * BW
        wide = [pl.ds(0, cut), pl.ds(cut, cols - cut)]
        pair = [pl.ds(0, 2), pl.ds(2, 2)]
        top, low = pl.ds(0, half), pl.ds(half, half)
        self.place, self.buf, self.fin, self.mid, self.fin_two = place, buf, fin, mid, fin_two
        far_two = [far_a, far_b]

        def views(h):
            def first(i, part):
                if h == 0:
                    return buf.at[i, pair[part], top, :]
                return buf.at[pair[part], i, low, :]

            def second(i, part):
                return mid.at[h, i, :, wide[part]]

            one = (
                first,
                lambda side: far.at[h, side],
                lambda side, part: fin.at[h, side, pair[part]],
            )
            two = (
                second,
                lambda side: far_two[side].at[h],
                lambda side, part: fin_two.at[h, side, :, wide[part]],
            )
            return one, two

        names = [("y", "x"), ("x", "y")]
        self.one, self.two = [], []
        for h in range(2):
            one, two = views(h)
            self.one.append(Scatter(net, place.axes[names[h][0]], *one))
            self.two.append(Scatter(net, place.axes[names[h][1]], *two))

    def start(self):
        for ring_ in self.one:
            ring_.start()

    def relay(self):
        for ring_ in self.one:
            ring_.relay()

    def turn(self):
        for h in range(2):
            self.one[h].finish()
            rows = pl.ds(h * self.half, self.half)

            def body(i, _):
                own = (
                    self.buf[self.place.y, i, rows, :]
                    if h == 0
                    else self.buf[i, self.place.x, rows, :]
                )
                self.mid[h, i] = total(own, self.fin[h, 0, i], self.fin[h, 1, i])
                return 0

            lax.fori_loop(0, 4, body, 0)
            self.two[h].start()

    def relay_two(self):
        for ring_ in self.two:
            ring_.relay()

    def finish(self, out):
        for h in range(2):
            self.two[h].finish()
            own = self.mid[h, self.place.x if h == 0 else self.place.y]
            rows = pl.ds(h * self.half, self.half)
            out[rows, :] = total(own, self.fin_two[h, 0], self.fin_two[h, 1])


def dot(left, right, dims=((1,), (0,))):
    return lax.dot_general(left, right, (dims, ((), ())), preferred_element_type=F32)


def pick_kernel(at_ref, have_ref, w_ref, out_ref):
    for child in range(2):
        for j in range(12):
            block = w_ref[:, pl.ds(pl.multiple_of(at_ref[child, j] * BW, BW), BW)]
            mine = block.astype(F32) * have_ref[child, j].astype(F32)
            out_ref[j // 3, child, :, pl.ds((j % 3) * BW, BW)] = mine.astype(BF16)


SENDS_ONE = 54


def first_kernel(
    pk, l_ref, f_ref, la, sa, sel, p, g_far, g_fin, own, s0, s1, s2, s3, s4, s5, send, recv
):
    place = Place()
    z = place.z
    place.meet(False)
    net = Net(send, recv)
    half = [pl.ds(0, 192), pl.ds(192, 192)]
    links = Gather(
        net,
        place.axes["z"],
        lambda i, part: la.at[i] if part is None else la.at[i, half[part]],
        own=l_ref,
    )
    picked = Scatter(
        net,
        place.axes["z"],
        lambda i, part: pk.at[i, part],
        lambda side: g_far.at[side],
        lambda side, part: g_fin.at[side, part],
    )
    spread = Gather(
        net,
        place.axes["z"],
        lambda i, part: sel.at[i] if part is None else sel.at[i, part],
    )
    reduced = GridScatter(net, place, p, [s0, s1, s2, s3, s4, s5])
    solved = GridGather(net, place, sa)

    def fill(q, source):
        def body(t, _):
            cols = pl.ds(pl.multiple_of(t * 512, 512), 512)
            part = dot(source[...], f_ref[:, cols]).astype(BF16)
            for k in range(4):
                p[q, k, :, cols] = part[96 * k : 96 * k + 96]
            return 0

        lax.fori_loop(0, 4, body, 0)

    links.start()
    la[z] = l_ref[...]
    fill(z, l_ref)
    links.relay()
    picked.start()
    fill(ring(z, 1), la.at[ring(z, 1)])
    fill(ring(z, 3), la.at[ring(z, 3)])
    links.finish()
    fill(ring(z, 2), la.at[ring(z, 2)])
    reduced.start()
    reduced.relay()
    picked.relay()
    reduced.turn()
    picked.finish()
    for child in range(2):
        sel[z, child] = total(pk[z, child], g_fin[0, child], g_fin[1, child])
    spread.start()
    reduced.relay_two()
    reduced.finish(own)
    sa[place.y, place.x] = own[...]
    solved.start()
    solved.relay()
    solved.turn()
    spread.relay()
    solved.relay_two()
    spread.finish()
    solved.finish()
    net.drain()


SENDS_TWO = 78


def second_kernel(
    sel, sa, f_ref, w_ref, pa, lf, out, mo, m_in, m4, block, mr, ap, d_far, d_fin, aj, gp, k_far,
    k_fin, s0, s1, s2, s3, s4, s5, send, recv,
):
    place = Place()
    x, y, z, core = place.x, place.y, place.z, place.core
    place.meet(True)
    net = Net(send, recv)
    half = [pl.ds(0, 48), pl.ds(48, 48)]
    tall = [pl.ds(0, 192), pl.ds(192, 192)]
    other = 1 - core
    swap = net.copy(mo, m_in, place.sibling)
    margin = GridScatter(net, place, m4, [s0, s1, s2, s3, s4, s5])
    margin_row = Gather(
        net,
        place.axes["z"],
        lambda i, part: mr.at[i] if part is None else mr.at[i, half[part]],
    )
    adjoint = Scatter(
        net,
        place.axes["z"],
        lambda i, part: ap.at[i, half[part]],
        lambda side: d_far.at[side],
        lambda side, part: d_fin.at[side, half[part]],
    )
    adjoint_all = GridGather(net, place, aj.at[core])
    adjoint_swap = net.copy(aj.at[core], aj.at[core], place.sibling)
    pulled = GridGather(net, place, pa)
    lifted = Gather(
        net,
        place.axes["z"],
        lambda i, part: lf.at[i] if part is None else lf.at[i, part],
    )
    grad = Scatter(
        net,
        place.axes["z"],
        lambda i, part: gp.at[i, tall[part]],
        lambda side: k_far.at[side],
        lambda side, part: k_fin.at[side, tall[part]],
    )

    def cross(q, _):
        part = dot(sel[q, other], sel[z, other], ((0,), (0,))).astype(BF16)
        for k in range(4):
            mo[q, k] = part[96 * k : 96 * k + 96]
        return 0

    lax.fori_loop(0, 4, cross, 0)
    swap.start()
    scaled = (sa[y, x].astype(F32) * w_ref[...]).astype(BF16)

    def adjoint_rows(q, _):
        right = sa[q].reshape(384, 2048)
        ap[q] = dot(scaled, right, ((1,), (1,))).astype(BF16)
        return 0

    lax.fori_loop(0, 4, adjoint_rows, 0)
    adjoint.start()
    swap.wait_recv()

    def same(q, _):
        part = dot(sel[q, core], sel[z, core], ((0,), (0,)))
        for k in range(4):
            m4[q, k] = (part[96 * k : 96 * k + 96] + m_in[q, k].astype(F32)).astype(BF16)
        return 0

    lax.fori_loop(0, 4, same, 0)
    margin.start()
    adjoint.relay()
    margin.relay()
    adjoint.finish()
    aj[core, y, x] = total(ap[z], d_fin[0], d_fin[1])
    margin.turn()
    adjoint_all.start()
    margin.relay_two()
    margin.finish(block)
    mr[z] = block[...]
    margin_row.start()
    adjoint_all.relay()
    margin_row.relay()
    margin_row.finish()

    def pull(t, _):
        cols = pl.ds(pl.multiple_of(t * 512, 512), 512)
        part = jnp.zeros((96, 512), F32)
        for q in range(4):
            part = part + dot(mr[q], sa[q, :, :, cols].reshape(384, 512))
        pa[y, x, :, cols] = (2.0 * part * w_ref[:, cols]).astype(BF16)
        return 0

    lax.fori_loop(0, 4, pull, 0)
    pulled.start()
    adjoint_all.turn()
    pulled.relay()
    adjoint_all.relay_two()
    adjoint_all.finish()
    adjoint_swap.start()

    def lift(child):
        part = jnp.zeros((384, 384), F32)
        for q in range(4):
            part = part + dot(sel[q, child], aj[child, q].reshape(384, 384))
        lf[z, child] = part.astype(BF16)

    lift(core)
    pulled.turn()
    adjoint_swap.wait_recv()
    lift(other)
    lifted.start()
    pulled.relay_two()
    lifted.relay()
    pulled.finish()

    def project(q, _):
        gp[q] = dot(pa[q].reshape(384, 2048), f_ref[...], ((1,), (1,))).astype(BF16)
        return 0

    lax.fori_loop(0, 4, project, 0)
    grad.start()
    grad.relay()
    lifted.finish()
    grad.finish()
    out[...] = total(gp[z], k_fin[0], k_fin[1])
    net.drain()


def place_kernel(at_ref, have_ref, w_ref, s_ref, lf_ref, out_ref):
    def body(b, _):
        cols = pl.ds(pl.multiple_of(b * BW, BW), BW)
        value = 2.0 * w_ref[:, cols].astype(F32) * s_ref[:, cols]
        for child in range(2):
            j = at_ref[child, b]
            third = pl.ds(pl.multiple_of(lax.rem(j, 3) * BW, BW), BW)
            part = lf_ref[j // 3, child, :, third].astype(F32)
            value = value + 2.0 * part * have_ref[child, b].astype(F32)
        out_ref[:, cols] = value.astype(BF16)
        return 0

    lax.fori_loop(0, 24, body, 0)


def shape(*dims):
    return jax.ShapeDtypeStruct(dims, BF16)


def local(root_inverse, child_inverse, coupling, child_weights, root_weights, parent_blocks):
    col_index = lax.axis_index("col")
    root_rows, root_cols = root_inverse.shape
    local_blocks = root_cols // BW
    offset = parent_blocks - col_index * local_blocks
    have = ((offset >= 0) & (offset < local_blocks)).astype(jnp.int32)
    at = jnp.clip(offset, 0, local_blocks - 1)
    match = offset[:, None, :] == jnp.arange(local_blocks, dtype=jnp.int32)[None, :, None]
    back_have = jnp.any(match, axis=2).astype(jnp.int32)
    back_at = jnp.sum(match * jnp.arange(12, dtype=jnp.int32)[None, None, :], axis=2)

    picked = pl.pallas_call(
        pick_kernel,
        out_shape=shape(4, 2, root_rows, 384),
        in_specs=[SMEM, SMEM, VMEM],
        out_specs=VMEM,
        name="pick",
    )(at, have, root_inverse)

    factor = child_inverse[0]
    weights = child_weights[0].astype(F32)[None, :]
    links_all, solved_all, selected = pl.pallas_call(
        first_kernel,
        out_shape=(shape(4, 384, 512), shape(4, 4, 96, 2048), shape(4, 2, 384, 384)),
        in_specs=[VMEM] * 3,
        out_specs=(VMEM,) * 3,
        scratch_shapes=[
            pltpu.VMEM((4, 4, 96, 2048), BF16),
            pltpu.VMEM((2, 384, 384), BF16),
            pltpu.VMEM((2, 2, 384, 384), BF16),
            pltpu.VMEM((96, 2048), BF16),
            *grid_scatter_scratch(96, 2048),
            pltpu.SemaphoreType.DMA((SENDS_ONE,)),
            pltpu.SemaphoreType.DMA((SENDS_ONE,)),
        ],
        compiler_params=pltpu.CompilerParams(collective_id=0, has_side_effects=True),
        name="solve",
    )(picked, coupling[0], factor)

    pulled_all, lifted_all, grad_links = pl.pallas_call(
        second_kernel,
        out_shape=(shape(4, 4, 96, 2048), shape(4, 2, 384, 384), shape(384, 512)),
        in_specs=[VMEM] * 4,
        out_specs=(VMEM,) * 3,
        scratch_shapes=[
            pltpu.VMEM((4, 4, 96, 384), BF16),
            pltpu.VMEM((4, 4, 96, 384), BF16),
            pltpu.VMEM((4, 4, 96, 384), BF16),
            pltpu.VMEM((96, 384), BF16),
            pltpu.VMEM((4, 96, 384), BF16),
            pltpu.VMEM((4, 96, 384), BF16),
            pltpu.VMEM((2, 48, 384), BF16),
            pltpu.VMEM((2, 96, 384), BF16),
            pltpu.VMEM((2, 4, 4, 96, 384), BF16),
            pltpu.VMEM((4, 384, 512), BF16),
            pltpu.VMEM((2, 192, 512), BF16),
            pltpu.VMEM((2, 384, 512), BF16),
            *grid_scatter_scratch(96, 384),
            pltpu.SemaphoreType.DMA((SENDS_TWO,)),
            pltpu.SemaphoreType.DMA((SENDS_TWO,)),
        ],
        compiler_params=pltpu.CompilerParams(collective_id=1, has_side_effects=True),
        name="pull",
    )(selected, solved_all, factor, weights)

    grad_root = pl.pallas_call(
        place_kernel,
        out_shape=shape(root_rows, root_cols),
        in_specs=[SMEM, SMEM, VMEM, VMEM, VMEM],
        out_specs=VMEM,
        name="place",
    )(back_at, back_have, root_inverse, root_weights.astype(F32)[None, :], lifted_all)

    grad_factor = jnp.dot(
        links_all.reshape(1536, 512).T,
        pulled_all.reshape(1536, 2048),
        preferred_element_type=F32,
    )
    grad_factor = (grad_factor + 2.0 * factor.astype(F32) * weights).astype(BF16)
    return (grad_root, grad_factor[None], grad_links[None])


def solution(mesh):
    return jax.shard_map(
        local,
        mesh=mesh,
        in_specs=(
            P(("grp", "row"), "col"),
            P("grp", "row", "col"),
            P("grp", "col", "row"),
            P("grp", "col"),
            P("col"),
            P(),
        ),
        out_specs=(P(("grp", "row"), "col"), P("grp", "row", "col"), P("grp", "col", "row")),
        check_vma=False,
    )
```

time: 579 us -> 223 us (0.39)
  waiting for transfers between devices: 468 us -> 0 us
  Pallas kernels: 0 us -> 208 us
  matrix products: 44.4 us -> 8.24 us
  local copies, waits for them, and re-layouts: 23.4 us -> 0.76 us
  between operations: 14.4 us -> 0.69 us
  blocking collectives: 13 us -> 0 us
  other arithmetic: 14.3 us -> 4.36 us
    reduce_scatter x4 -> x0, waiting for transfers between devices: 219 us -> none  [the longest x1 94.8 us: local(): lax.psum_scatter(jnp.dot(links_all, factor, preferred_element_type=jnp.fl...]
    pallas_call x0 -> x4, Pallas kernels: none -> 208 us  [the longest x1 104 us: local(): pl.pallas_call(first_kernel, out_shape=(shape(4, 384, 512), shape(4, 4, 9...]
    all_gather x5 -> x0, waiting for transfers between devices: 187 us -> none  [the longest x1 59.3 us: local(): pulled_all = lax.all_gather(pulled, 'row', axis=0, tiled=True)]
    psum x1 -> x0, waiting for transfers between devices: 60 us -> none  [local(): selected = lax.psum(picked.astype(jnp.bfloat16), 'col')]
    dot_general x13 -> x1, matrix products: 44.4 us -> 8.24 us  [local(): jnp.dot(links_all.reshape(1536, 512).T, pulled_all.reshape(1536, 2048), p...]
    unnamed x37 -> x9, local copies, waits for them, and re-layouts: 14.7 us -> 0.76 us
    all_gather x1 -> x0, blocking collectives: 13 us -> none  [local(): margin_row = lax.all_gather(margin, 'col', axis=1, tiled=True)]
  transfers between devices with their start and end apart: 10 -> 0, of which waited for: 10 -> 0; matrix products, arithmetic and copies ran while one was open for 11% -> 0% of each run, Pallas kernels for 0% -> 0%
where the time goes in v1:
time: 223 us; the launch traced here: 222 us
  Pallas kernels  208 us (93%)
  matrix products  8.24 us (4%)
  other arithmetic  4.36 us (2%)
    pallas_call x1, Pallas kernels, local(): pl.pallas_call(first_kernel, out_shape=(shape(4, 384, 512), shape(4, 4, 9...  104 us
    pallas_call x1, Pallas kernels, local(): pl.pallas_call(second_kernel, out_shape=(shape(4, 4, 96, 2048), shape(4,...  95.1 us
    dot_general x1, matrix products, local(): jnp.dot(links_all.reshape(1536, 512).T, pulled_all.reshape(1536, 2048), p...  8.24 us
    pallas_call x1, Pallas kernels, local(): pl.pallas_call(place_kernel, out_shape=shape(root_rows, root_cols), in_sp...  5.99 us

profile of v1, /device:TPU:0, one launch (start us, length us, event | category | flops | bytes accessed | tf_op | source)
XLA Modules:
  0.0 222.4 jit_solution(9620755718587524314)
XLA Ops:
  0.6 1.2 and_convert_fusion
  1.9 0.6 broadcast_clamp_fusion.at_ref
  2.4 3.7 %pick.1.pk = bf16[4,2,384,384]{3,2,1,0:T(8,128)(2,1)} custom-call(s32[2,12]{1,0:T(2,128)} %broadcast_clamp_fusion.at_ref, s32[2,12]{1,0:T(2,128)} %get-tuple-element.15.have_ref, bf16[384,3072]{1,0:T(8,128)(2,1)} %w_ref.3), custom_call_target="tpu_custom_call" | custom-call | tf_op jit(solution)/shard_map/pick/pallas_call | solution.py:527
  6.1 0.0 copy-start.2
  6.1 103.6 %solve.1 = (bf16[4,384,512]{2,1,0:T(8,128)(2,1)}, bf16[4,4,96,2048]{3,2,1,0:T(8,128)(2,1)}, bf16[4,2,384,384]{3,2,1,0:T(8,128)(2,1)}) custom-call(bf16[4,2,384,384]{3,2,1,0:T(8,128)(2,1)} %pick.1.pk, bf16[384,512]{1,0:T(8,128)(2,1)} %bitcast.14, bf16[512,2048]{1,0:T(8,128)(2,1)} %bitcast.12), custom_call_target="tpu_custom_call" | custom-call | tf_op jit(solution)/shard_map/solve/pallas_call | solution.py:537
  109.8 0.0 copy-done.2
  109.8 0.6 convert_element_type.20.w_ref
  110.4 0.0 copy-start
  110.4 95.1 %pull.1 = (bf16[4,4,96,2048]{3,2,1,0:T(8,128)(2,1)}, bf16[4,2,384,384]{3,2,1,0:T(8,128)(2,1)}, bf16[384,512]{1,0:T(8,128)(2,1)}) custom-call(bf16[4,2,384,384]{3,2,1,0:T(8,128)(2,1)} %get-tuple-element.9.sel, bf16[4,4,96,2048]{3,2,1,0:T(8,128)(2,1)} %get-tuple-element.10.sa, bf16[512,2048]{1,0:T(8,128)(2,1)} %bitcast.13, f32[1,2048]{1,0:T(1,128)} %convert_element_type.20.w_ref), custom_call_target="tpu_custom_call" | custom-call | tf_op jit(solution)/shard_map/pull/pallas_call | solution.py:555
  205.5 0.0 copy-done
  205.5 0.0 copy-start.3
  205.5 8.2 %fusion = bf16[1,512,2048]{2,1,0:T(8,128)(2,1)} fusion(bf16[1536,512]{1,0:T(8,128)(2,1)} %bitcast.19, bf16[1536,2048]{1,0:T(8,128)(2,1)} %bitcast.18, f32[2048]{0:T(1024)S(1)} %bitcast.17, bf16[1,512,2048]{2,1,0:T(8,128)(2,1)S(1)} %copy-done), kind=kOutput, calls=%fused_computation.1 | convolution fusion | flops 3225419776 | bytes 12066816 | tf_op jit(solution)/shard_map/dot_general | solution.py:589
  213.8 0.1 fusion.1
  213.8 0.6 convert_element_type.18.have_ref
  214.4 0.6 select_reduce_fusion.at_ref
  215.1 0.0 copy-done.3
  215.1 0.6 broadcast_in_dim.19
  215.7 0.0 copy-start.1
  215.7 6.0 %place.1 = bf16[384,3072]{1,0:T(8,128)(2,1)} custom-call(s32[2,24]{1,0:T(2,128)} %select_reduce_fusion.at_ref, s32[2,24]{1,0:T(2,128)} %convert_element_type.18.have_ref, bf16[384,3072]{1,0:T(8,128)(2,1)} %w_ref.3, f32[1,3072]{1,0:T(1,128)} %bitcast.16, bf16[4,2,384,384]{3,2,1,0:T(8,128)(2,1)} %get-tuple-element.11.lf_ref), custom_call_target="tpu_custom_call" | custom-call | tf_op jit(solution)/shard_map/place/pallas_call | solution.py:581
  221.7 0.0 copy-done.1
  221.7 0.7 copy.12
  (1 shorter events, 0.0 us)
Async XLA Ops:
  6.1 103.6 %copy-start.2 = (bf16[1,2048]{1,0:T(2,128)(2,1)S(1)}, bf16[1,2048]{1,0:T(2,128)(2,1)}, u32[]{:S(2)}) copy-start(bf16[1,2048]{1,0:T(2,128)(2,1)} %param.9) | copy-start | bytes 12292
  110.4 95.1 %copy-start = (bf16[1,512,2048]{2,1,0:T(8,128)(2,1)S(1)}, bf16[1,512,2048]{2,1,0:T(8,128)(2,1)}, u32[]{:S(2)}) copy-start(bf16[1,512,2048]{2,1,0:T(8,128)(2,1)} %param.7) | copy-start | bytes 6291460
  205.5 9.6 %copy-start.3 = (bf16[3072]{0:T(1024)(128)(2,1)S(1)}, bf16[3072]{0:T(1024)(128)(2,1)}, u32[]{:S(2)}) copy-start(bf16[3072]{0:T(1024)(128)(2,1)} %param.10) | copy-start | bytes 18436
  215.7 6.0 %copy-start.1 = (bf16[384,512]{1,0:T(8,128)(2,1)S(1)}, bf16[384,512]{1,0:T(8,128)(2,1)}, u32[]{:S(2)}) copy-start(bf16[384,512]{1,0:T(8,128)(2,1)} %get-tuple-element.14) | copy-start | bytes 1179652
